TPU v7x, 32 devices: a whole 2x2x4 slice. The times are simulated.
32 devices in a mesh: expert: 4 (over y, core), dp: 8 (over z, x).
Axes of the slice: x: 2, y: 2, z: 4, core: 2. Of those that a mesh axis runs over, the one named last changes fastest.
Arguments:
- tokens: bfloat16 [4096, 1024], P(('expert', 'dp')), may hold values from -6 to 6
- d_output: bfloat16 [4096, 1024], P(('expert', 'dp')), may hold values from -6 to 6
- expert_ids: int32 [4096, 8], P(('expert', 'dp')), may hold values from 0 to 127, as said below
- gate_scores: bfloat16 [4096, 8], P(('expert', 'dp')), may hold values from 0.099609375 to 1
- gate_up_w: bfloat16 [4, 1024, 768], P('expert', 'dp'), may hold values from -0.1875 to 0.1875
- down_w: bfloat16 [4, 1024, 384], P('expert', 'dp'), may hold values from -0.3125 to 0.3125
Outputs:
- d_tokens: bfloat16 [4096, 1024], P(('expert', 'dp'))
- d_gates: bfloat16 [4096, 8], P(('expert', 'dp'))
- d_down: float32 [4, 1024, 384], P('expert', 'dp')
Inputs may be any that keep to these rules, and one draw needn't show every extreme that they name: `expert_ids`: each token names 8 different experts. The tokens of one device name no expert more than 12 times, and in every draw one expert below 4 is named exactly 12 times by the tokens of every device.
All inputs are finite; a program needn't handle non-finite values.
Results may differ from a plain program's by a relative error of at most 0.0062.
Values may be sent and summed in bfloat16 or wider, within the bound.
A program may use at most 64 MiB of HBM per device.

v0:
```python
import jax
import jax.numpy as jnp
from jax import lax
from jax.sharding import PartitionSpec as P

TOPK = 8
CAP = 12


def transpose_product(left, right):
    return lax.dot_general(
        left, right, (((0,), (0,)), ((), ())), preferred_element_type=jnp.float32
    )


def product_transposed(left, right):
    return lax.dot_general(
        left, right, (((1,), (1,)), ((), ())), preferred_element_type=jnp.float32
    )


def on_device(tokens, d_output, expert_ids, gate_scores, gate_up_w, down_w):
    gate_full, down_full = (
        lax.all_gather(gate_up_w, "dp", axis=1, tiled=True),
        lax.all_gather(down_w, "dp", axis=1, tiled=True),
    )
    gate_full = gate_full[0]
    down_full = down_full[0]
    groups = lax.axis_size("expert")
    slot_count = groups * CAP
    tok_rows = tokens.shape[0]
    features = tokens.shape[1]
    width = down_w.shape[2]
    flat_ids = expert_ids.reshape(-1)
    entries = flat_ids.shape[0]
    one_hot = (flat_ids[:, None] == jnp.arange(groups, dtype=jnp.int32)[None, :]).astype(jnp.int32)
    earlier = jnp.cumsum(one_hot, axis=0) - one_hot
    within = jnp.sum(earlier * one_hot, axis=1)
    inside = flat_ids < groups
    slot_of = jnp.where(inside, flat_ids * CAP + within, slot_count)
    owner = (
        jnp.full((slot_count,), -1, jnp.int32)
        .at[slot_of]
        .set(jnp.arange(entries, dtype=jnp.int32), mode="drop")
    )
    filled = owner >= 0
    source = jnp.maximum(owner, 0)
    token_of = jnp.where(filled, source // TOPK, -1)
    picker = (token_of[:, None] == jnp.arange(tok_rows, dtype=jnp.int32)[None, :]).astype(
        jnp.bfloat16
    )
    send_inputs = jnp.dot(picker, tokens, preferred_element_type=jnp.float32).astype(jnp.bfloat16)
    send_upstream = jnp.dot(picker, d_output, preferred_element_type=jnp.float32).astype(
        jnp.bfloat16
    )
    send_gates = jnp.where(filled, gate_scores.reshape(-1)[source], jnp.zeros((), jnp.bfloat16))
    recv_inputs, recv_upstream, recv_gates = (
        lax.all_to_all(
            send_inputs.reshape(groups, CAP, features),
            "expert",
            split_axis=0,
            concat_axis=0,
            tiled=True,
        ),
        lax.all_to_all(
            send_upstream.reshape(groups, CAP, features),
            "expert",
            split_axis=0,
            concat_axis=0,
            tiled=True,
        ),
        lax.all_to_all(
            send_gates.reshape(groups, CAP), "expert", split_axis=0, concat_axis=0, tiled=True
        ),
    )
    slot_inputs = recv_inputs.reshape(slot_count, features)
    slot_upstream = recv_upstream.reshape(slot_count, features)
    slot_gates = recv_gates.reshape(slot_count).astype(jnp.float32)
    pre_act = jnp.dot(slot_inputs, gate_full, preferred_element_type=jnp.float32)
    gate_part = pre_act[:, :width]
    up_part = pre_act[:, width:]
    sigma = jax.nn.sigmoid(gate_part)
    activ = gate_part * sigma
    hidden = (activ * up_part).astype(jnp.bfloat16)
    expert_out = product_transposed(hidden, down_full)
    upstream_float = slot_upstream.astype(jnp.float32)
    slot_grad = jnp.sum(upstream_float * expert_out, axis=1).astype(jnp.bfloat16)
    d_expert_out = (slot_gates[:, None] * upstream_float).astype(jnp.bfloat16)
    d_hidden = jnp.dot(d_expert_out, down_full, preferred_element_type=jnp.float32)
    d_gate_part = d_hidden * up_part * sigma * (1.0 + gate_part * (1.0 - sigma))
    d_up_part = d_hidden * activ
    d_pre = jnp.concatenate([d_gate_part, d_up_part], axis=1).astype(jnp.bfloat16)
    d_slot = product_transposed(d_pre, gate_full).astype(jnp.bfloat16)
    down_share = lax.psum_scatter(
        transpose_product(d_expert_out, hidden), "dp", scatter_dimension=0, tiled=True
    )
    back_rows, back_grads = (
        lax.all_to_all(
            d_slot.reshape(groups, CAP, features), "expert", split_axis=0, concat_axis=0, tiled=True
        ),
        lax.all_to_all(
            slot_grad.reshape(groups, CAP), "expert", split_axis=0, concat_axis=0, tiled=True
        ),
    )
    back_rows = back_rows.reshape(slot_count, features)
    back_grads = back_grads.reshape(slot_count)
    grad_tokens = transpose_product(picker, back_rows).astype(jnp.bfloat16)
    gathered_grads = back_grads[jnp.minimum(slot_of, slot_count - 1)]
    grad_gates = jnp.where(inside, gathered_grads, jnp.zeros((), jnp.bfloat16)).reshape(
        tok_rows, TOPK
    )
    return (grad_tokens, grad_gates, down_share[None])


def solution(mesh):
    return jax.shard_map(
        on_device,
        mesh=mesh,
        in_specs=(
            P(("expert", "dp"), None),
            P(("expert", "dp"), None),
            P(("expert", "dp"), None),
            P(("expert", "dp"), None),
            P("expert", "dp", None),
            P("expert", "dp", None),
        ),
        out_specs=(P(("expert", "dp"), None), P(("expert", "dp"), None), P("expert", "dp", None)),
        check_vma=False,
    )
```

profile of v0, /device:TPU:0, one launch (start us, length us, event | category | flops | bytes accessed | tf_op | source)
XLA Modules:
  0.0 151.2 jit_solution(2846326151058442494)
XLA Ops:
  7.9 0.8 copy.23
  8.8 1.1 reduce-window.6
  10.6 0.7 broadcast_multiply_fusion
  11.5 0.8 copy.27
  12.5 4.3 %scatter_custom_fusion = s32[48]{0:T(128)S(1)} fusion(s32[1024]{0:T(1024)S(1)} %bitcast.96, s32[1024]{0:T(1024)S(1)} %iota.15, s32[]{:T(128)} %constant.14.clone.1), kind=kCustom, calls=%fused_computation.100 | custom fusion | bytes 196 | tf_op jit(solution)/shard_map/scatter | solution.py:44
  16.9 0.8 gather_fusion
  18.3 4.3 %all-to-all-start = ((bf16[4,1,12]{2,1,0:T(2,128)(2,1)}), bf16[4,1,12]{2,1,0:T(2,128)(2,1)S(1)}, u32[]{:S(2)}, u32[]{:S(2)}) async-start(bf16[4,1,12]{2,1,0:T(2,128)(2,1)} %all_to_all.25), calls=%async_computation | async-start | bytes 4096 | tf_op jit(solution)/shard_map/all_to_all | solution.py:72
  23.7 34.6 %all_gather.6 = bf16[1,1024,384]{2,1,0:T(8,128)(2,1)S(1)} all-gather(bf16[1,128,384]{2,1,0:T(8,128)(2,1)S(1)} %copy-done.3), channel_id=1, replica_groups=mesh['expert'=4,'dp'=8] {'dp'}, dimensions={1}, use_global_device_ids=true | all-gather | bytes 884736 | tf_op jit(solution)/shard_map/all_gather | solution.py:25
  59.0 3.3 %all-to-all-start.1 = ((bf16[4,12,1024]{2,1,0:T(8,128)(2,1)}), bf16[4,12,1024]{2,1,0:T(8,128)(2,1)S(1)}, u32[]{:S(2)}, u32[]{:S(2)}) async-start(bf16[4,12,1024]{2,1,0:T(8,128)(2,1)} %reshape.156), calls=%async_computation.1 | async-start | bytes 262144 | tf_op jit(solution)/shard_map/all_to_all | solution.py:65
  62.5 4.5 %all-to-all-done.1 = bf16[4,12,1024]{2,1,0:T(8,128)(2,1)S(1)} async-done(((bf16[4,12,1024]{2,1,0:T(8,128)(2,1)}), bf16[4,12,1024]{2,1,0:T(8,128)(2,1)S(1)}, u32[]{:S(2)}, u32[]{:S(2)}) %all-to-all-start.1) | async-done | bytes 98336 | tf_op jit(solution)/shard_map/all_to_all | solution.py:65
  66.9 3.3 %all-to-all-start.2 = ((bf16[4,12,1024]{2,1,0:T(8,128)(2,1)}), bf16[4,12,1024]{2,1,0:T(8,128)(2,1)S(1)}, u32[]{:S(2)}, u32[]{:S(2)}) async-start(bf16[4,12,1024]{2,1,0:T(8,128)(2,1)} %reshape.157), calls=%async_computation.2 | async-start | bytes 262144 | tf_op jit(solution)/shard_map/all_to_all | solution.py:58
  70.5 4.4 %all-to-all-done.2 = bf16[4,12,1024]{2,1,0:T(8,128)(2,1)S(1)} async-done(((bf16[4,12,1024]{2,1,0:T(8,128)(2,1)}), bf16[4,12,1024]{2,1,0:T(8,128)(2,1)S(1)}, u32[]{:S(2)}, u32[]{:S(2)}) %all-to-all-start.2) | async-done | bytes 98336 | tf_op jit(solution)/shard_map/all_to_all | solution.py:58
  74.9 1.8 %fusion.2 = f32[48,768]{1,0:T(8,128)S(1)} fusion(bf16[48,1024]{1,0:T(8,128)(2,1)S(1)} %reshape.158, bf16[1,1024,768]{2,1,0:T(8,128)(2,1)} %all-gather.2.cloned.1.call-done), kind=kOutput, calls=%fused_computation.4 | convolution fusion | flops 75497472 | bytes 1818624 | tf_op jit(solution)/shard_map/dot_general | solution.py:79
  76.9 1.6 %fusion.11 = f32[1024,384]{1,0:T(8,128)} fusion(bf16[48,384]{1,0:T(8,128)(2,1)S(1)} %get-tuple-element.57, f32[48,1024]{1,0:T(8,128)S(1)} %reshape.163, f32[48]{0:T(128)S(1)} %reshape.164), kind=kOutput, calls=%fused_computation.17 | convolution fusion | flops 37847040 | bytes 1806528 | tf_op jit(solution)/shard_map/dot_general | solution.py:11
  79.7 3.2 %all-to-all-start.4 = ((bf16[4,1,12]{2,1,0:T(2,128)(2,1)}), bf16[4,1,12]{2,1,0:T(2,128)(2,1)S(1)}, u32[]{:S(2)}, u32[]{:S(2)}) async-start(bf16[4,1,12]{2,1,0:T(2,128)(2,1)} %convert_element_type.93), calls=%async_computation.4 | async-start | bytes 4096 | tf_op jit(solution)/shard_map/all_to_all | solution.py:101
  84.2 2.4 %all-to-all-done.4 = bf16[4,1,12]{2,1,0:T(2,128)(2,1)S(1)} async-done(((bf16[4,1,12]{2,1,0:T(2,128)(2,1)}), bf16[4,1,12]{2,1,0:T(2,128)(2,1)S(1)}, u32[]{:S(2)}, u32[]{:S(2)}) %all-to-all-start.4) | async-done | bytes 128 | tf_op jit(solution)/shard_map/all_to_all | solution.py:101
  86.6 3.3 %all-to-all-start.3 = ((bf16[4,12,1024]{2,1,0:T(8,128)(2,1)}), bf16[4,12,1024]{2,1,0:T(8,128)(2,1)S(1)}, u32[]{:S(2)}, u32[]{:S(2)}) async-start(bf16[4,12,1024]{2,1,0:T(8,128)(2,1)} %reshape.159), calls=%async_computation.3 | async-start | bytes 262144 | tf_op jit(solution)/shard_map/all_to_all | solution.py:98
  90.1 0.7 fusion.30
  90.8 0.7 fusion.28
  91.5 0.7 fusion.29
  92.2 4.4 %fusion.24 = (bf16[1024]{0:T(1024)(128)(2,1)S(1)}, s32[1024,1]{0,1:T(1,128)S(1)}) fusion(bf16[]{:T(256)} %bitcast.47, bf16[]{:T(256)} %bitcast.48, bf16[]{:T(256)} %bitcast.49, bf16[]{:T(256)} %bitcast.50, bf16[]{:T(256)} %bitcast.51, bf16[]{:T(256)} %bitcast.53, bf16[]{:T(256)} %bitcast.52, pred[1024,1]{0,1:T(4,128)(4,1)S(1)} %lt.44, ...), kind=kLoop, calls=%fused_computation.93 | loop fusion | flops 18432 | bytes 15374 | tf_op jit(solution)/shard_map/gather | solution.py:108
  97.1 25.7 %select_select_fusion = bf16[1024]{0:T(1024)(128)(2,1)S(1)} fusion(pred[1024]{0:T(1024)(128)(4,1)S(1)} %get-tuple-element.52, pred[1024]{0:T(1024)(128)(4,1)S(1)} %get-tuple-element.51, pred[1024]{0:T(1024)(128)(4,1)S(1)} %get-tuple-element.50, pred[1024]{0:T(1024)(128)(4,1)S(1)} %get-tuple-element.49, pred[1024]{0:T(1024)(128)(4,1)S(1)} %get-tuple-element.48, ...), kind=kLoop, calls=%fused_computation.94 | loop fusion | flops 41984 | bytes 46162 | tf_op jit(solution)/shard_map/gather | solution.py:108
  123.6 1.0 convolution_convert_fusion
  124.7 19.6 %reduce-scatter.2.cloned.1.call-done = f32[128,384]{1,0:T(8,128)} async-done(((f32[1024,384]{1,0:T(8,128)}), f32[128,384]{1,0:T(8,128)}) %reduce-scatter.2.cloned.1.call-update) | async-done | bytes 196624 | tf_op jit(solution)/shard_map/reduce_scatter | solution.py:94
  (56 shorter events, 8.7 us)
Async XLA Ops:
  7.2 15.4 %copy-start = (bf16[128,1024]{1,0:T(8,128)(2,1)S(1)}, bf16[128,1024]{1,0:T(8,128)(2,1)}, u32[]{:S(2)}) copy-start(bf16[128,1024]{1,0:T(8,128)(2,1)} %param.7) | copy-start | bytes 786436
  7.2 16.3 %copy-start.2 = (bf16[128,1024]{1,0:T(8,128)(2,1)S(1)}, bf16[128,1024]{1,0:T(8,128)(2,1)}, u32[]{:S(2)}) copy-start(bf16[128,1024]{1,0:T(8,128)(2,1)} %param.6) | copy-start | bytes 786436
  7.2 16.6 %copy-start.3 = (bf16[1,128,384]{2,1,0:T(8,128)(2,1)S(1)}, bf16[1,128,384]{2,1,0:T(8,128)(2,1)}, u32[]{:S(2)}) copy-start(bf16[1,128,384]{2,1,0:T(8,128)(2,1)} %param.11) | copy-start | bytes 294916
  7.2 67.7 %all-gather.2.cloned.1.call-start = ((), (), s32[]{:S(2)}) async-start(), calls=%async_computation.6 | async-start | bytes 1769472 | tf_op jit(solution)/shard_map/all_gather | solution.py:24
  18.3 40.7 %all-to-all-start = ((bf16[4,1,12]{2,1,0:T(2,128)(2,1)}), bf16[4,1,12]{2,1,0:T(2,128)(2,1)S(1)}, u32[]{:S(2)}, u32[]{:S(2)}) async-start(bf16[4,1,12]{2,1,0:T(2,128)(2,1)} %all_to_all.25), calls=%async_computation | async-start | bytes 4096 | tf_op jit(solution)/shard_map/all_to_all | solution.py:72
  59.0 7.9 %all-to-all-start.1 = ((bf16[4,12,1024]{2,1,0:T(8,128)(2,1)}), bf16[4,12,1024]{2,1,0:T(8,128)(2,1)S(1)}, u32[]{:S(2)}, u32[]{:S(2)}) async-start(bf16[4,12,1024]{2,1,0:T(8,128)(2,1)} %reshape.156), calls=%async_computation.1 | async-start | bytes 262144 | tf_op jit(solution)/shard_map/all_to_all | solution.py:65
  66.9 7.9 %all-to-all-start.2 = ((bf16[4,12,1024]{2,1,0:T(8,128)(2,1)}), bf16[4,12,1024]{2,1,0:T(8,128)(2,1)S(1)}, u32[]{:S(2)}, u32[]{:S(2)}) async-start(bf16[4,12,1024]{2,1,0:T(8,128)(2,1)} %reshape.157), calls=%async_computation.2 | async-start | bytes 262144 | tf_op jit(solution)/shard_map/all_to_all | solution.py:58
  70.3 74.0 %reduce-scatter.2.cloned.1.call-start = ((), (), s32[]{:S(2)}) async-start(), calls=%async_computation.7 | async-start | bytes 1769472 | tf_op jit(solution)/shard_map/reduce_scatter | solution.py:94
  78.6 4.4 %copy-start.1 = (bf16[1,1024,768]{2,1,0:T(8,128)(2,1)S(1)}, bf16[1,1024,768]{2,1,0:T(8,128)(2,1)}, u32[]{:S(2)}) copy-start(bf16[1,1024,768]{2,1,0:T(8,128)(2,1)} %all-gather.2.cloned.1.call-done) | copy-start | bytes 4718596
  79.7 6.9 %all-to-all-start.4 = ((bf16[4,1,12]{2,1,0:T(2,128)(2,1)}), bf16[4,1,12]{2,1,0:T(2,128)(2,1)S(1)}, u32[]{:S(2)}, u32[]{:S(2)}) async-start(bf16[4,1,12]{2,1,0:T(2,128)(2,1)} %convert_element_type.93), calls=%async_computation.4 | async-start | bytes 4096 | tf_op jit(solution)/shard_map/all_to_all | solution.py:101
  86.6 37.0 %all-to-all-start.3 = ((bf16[4,12,1024]{2,1,0:T(8,128)(2,1)}), bf16[4,12,1024]{2,1,0:T(8,128)(2,1)S(1)}, u32[]{:S(2)}, u32[]{:S(2)}) async-start(bf16[4,12,1024]{2,1,0:T(8,128)(2,1)} %reshape.159), calls=%async_computation.3 | async-start | bytes 262144 | tf_op jit(solution)/shard_map/all_to_all | solution.py:98
Sparse Core Ops, SparseCore 0:
  10.2 53.7 all-gather.1
  78.7 65.5 reduce-scatter.1
where the time goes:
time: 152 us; the launch traced here: 151 us
  blocking collectives  34.6 us (23%)
  other arithmetic  32.9 us (22%)
  waiting for transfers between devices  31.6 us (21%)
  starting transfers between devices  17.5 us (12%)
  between operations  14.3 us (9%)
  local copies, waits for them, and re-layouts  14.1 us (9%)
  matrix products  6.16 us (4%)
    all_gather x1, blocking collectives, on_device(): lax.all_gather(down_w, 'dp', axis=1, tiled=True)  34.6 us
    gather x3, other arithmetic, on_device(): gathered_grads = back_grads[jnp.minimum(slot_of, slot_count - 1)]  30.6 us
    reduce_scatter x1, waiting for transfers between devices, on_device(): lax.psum_scatter(transpose_product(d_expert_out, hidden), 'dp', scatter_d...  19.6 us
    all_to_all x1, waiting for transfers between devices, on_device(): lax.all_to_all(send_upstream.reshape(groups, CAP, features), 'expert', sp...  4.46 us
    all_to_all x1, waiting for transfers between devices, on_device(): lax.all_to_all(send_inputs.reshape(groups, CAP, features), 'expert', spli...  4.36 us
    scatter x1, local copies, waits for them, and re-layouts, on_device(): owner = jnp.full((slot_count,), -1, jnp.int32).at[slot_of].set(jnp.arange...  4.3 us
    all_to_all x1, starting transfers between devices, on_device(): lax.all_to_all(send_gates.reshape(groups, CAP), 'expert', split_axis=0, c...  4.26 us
    all_to_all x1, starting transfers between devices, on_device(): lax.all_to_all(send_upstream.reshape(groups, CAP, features), 'expert', sp...  3.33 us
  transfers between devices with their start and end apart: 7, of which 4 were waited for; matrix products, arithmetic and copies ran while one was open for 32% of the time, Pallas kernels for 0%

commit v1 on v0

v1 whole, which is shorter than its diff:
```python
import functools

import jax
import jax.numpy as jnp
from jax import lax
from jax.experimental import pallas as pl
from jax.experimental.pallas import tpu as pltpu
from jax.sharding import PartitionSpec as P

CAP = 12
PAD = 16
LANES = 128
BF = jnp.bfloat16
F32 = jnp.float32


def dot(left, right, dims=((1,), (0,))):
    return lax.dot_general(left, right, (dims, ((), ())), preferred_element_type=F32)


def kernel(groups, outer, inner, tok, dout, ids, scores, gate_in, down_in,
           o_tok, o_gates, o_down,
           gate_buf, down_buf, send, recv, hid_buf, dx_send, dx_buf, ret, back,
           w_send, w_recv, own_sem, s_send, s_recv, h_send, h_recv, x_send, x_recv, b_send, b_recv):
    n = outer * inner
    me = lax.axis_index("dp")
    mine = lax.axis_index("expert")
    zo = me // inner
    xi = me - zo * inner
    slots = groups * PAD
    rows = gate_in.shape[1]
    feats = tok.shape[1]
    width = down_in.shape[2]
    ins = (down_in, gate_in)
    bufs = (down_buf, gate_buf)

    barrier = pltpu.get_barrier_semaphore()
    for k in range(1, n):
        pl.semaphore_signal(barrier, inc=1, device_id={"dp": lax.rem(me + k, n)},
                            device_id_type=pl.DeviceIdType.MESH)
    for k in range(1, groups):
        pl.semaphore_signal(barrier, inc=1, device_id={"expert": lax.rem(mine + k, groups)},
                            device_id_type=pl.DeviceIdType.MESH)
    pl.semaphore_wait(barrier, n - 1 + groups - 1)

    def remote(src, dst, ss, rs, **where):
        return pltpu.make_async_remote_copy(
            src_ref=src, dst_ref=dst, send_sem=ss, recv_sem=rs,
            device_id=where, device_id_type=pl.DeviceIdType.MESH)

    def target(way):
        return me + (inner, -inner, 1, -1)[way]

    def can(way):
        return (zo < outer - 1, zo > 0, xi < inner - 1, xi > 0)[way]

    def hop(w, s, way, own=False):
        src = ins[w].at[0] if own else bufs[w].at[s]
        return remote(src, bufs[w].at[s], w_send.at[w, way, s], w_recv.at[w, s], dp=target(way))

    started = []

    def forward(s, way, valid, own=False):
        ok = can(way) if valid is None else jnp.logical_and(can(way), valid)

        @pl.when(ok)
        def _():
            for w in range(2):
                hop(w, s, way, own).start()
        started.append((ok, s, way, own))

    def arrive(s, valid):
        @pl.when(valid)
        def _():
            for w in range(2):
                hop(w, s, 0).wait_recv()

    for way in range(4):
        forward(me, way, None, own=True)
    own = [pltpu.make_async_copy(ins[w].at[0], bufs[w].at[me], own_sem.at[w]) for w in range(2)]
    for c in own:
        c.start()

    t_rows = tok.shape[0]
    topk = ids.shape[1]
    col = lax.broadcasted_iota(jnp.int32, (t_rows, slots), 1)
    col_e = col // PAD
    col_r = (col - col_e * PAD).astype(F32)
    idv = ids[...]
    scv = scores[...].astype(F32)
    live = jnp.zeros((t_rows, slots), F32)
    gcol = jnp.zeros((t_rows, slots), F32)
    hits = []
    for k in range(topk):
        hit = idv[:, k:k + 1] == col_e
        hits.append(hit)
        live = jnp.where(hit, 1.0, live)
        gcol = jnp.where(hit, scv[:, k:k + 1], gcol)
    lower = (lax.broadcasted_iota(jnp.int32, (t_rows, t_rows), 1)
             < lax.broadcasted_iota(jnp.int32, (t_rows, t_rows), 0))
    rank = dot(jnp.where(lower, 1.0, 0.0).astype(BF), live.astype(BF))
    pick = jnp.where(rank == col_r, live, 0.0)
    pick_t = jnp.transpose(pick).astype(BF)
    gate_t = jnp.transpose(pick * gcol)
    send[:, :feats] = dot(pick_t, tok[...]).astype(BF)
    send[:, feats:2 * feats] = dot(pick_t, dout[...]).astype(BF)
    send[:, 2 * feats:] = jnp.broadcast_to(
        jnp.sum(gate_t, axis=1, keepdims=True), (slots, LANES)).astype(BF)

    def block(e):
        return pl.ds(pl.multiple_of(e * PAD, PAD), PAD)

    def swap(src, dst, ss, rs, k):
        e = lax.rem(mine + k, groups)
        return remote(src.at[block(e), :], dst.at[block(mine), :], ss.at[k], rs.at[k], expert=e)

    for k in range(1, groups):
        swap(send, recv, s_send, s_recv, k).start()
    recv[block(mine), :] = send[block(mine), :]

    def peer(src, dst, ss, rs, k, sliced):
        d = lax.rem(me + k, n)
        return remote(src.at[d] if sliced else src.at[me], dst.at[me], ss.at[k], rs.at[k], dp=d)

    def outer_step(d):
        for way, s, valid in ((0, me - d * inner, zo >= d), (1, me + d * inner, zo + d < outer)):
            arrive(s, valid)
            for go in (way, 2, 3):
                forward(s, go, valid)

    outer_step(1) if outer > 1 else None

    for k in range(1, groups):
        swap(send, recv, s_send, s_recv, k).wait_recv()
    gates = recv[:, 2 * feats:2 * feats + 1].astype(F32)
    upstream = recv[:, feats:2 * feats]
    dexp = (gates * upstream.astype(F32)).astype(BF)
    for d in range(n):
        dx_send[d] = dexp[:, d * rows:(d + 1) * rows]
    for k in range(1, n):
        peer(dx_send, dx_buf, x_send, x_recv, k, True).start()
    dx_buf[me] = dx_send[me]

    for d in range(2, outer):
        outer_step(d)
    for di in range(1, inner):
        for d in range(outer):
            for sign in ((1,) if d == 0 else (-1, 1)):
                so = zo + sign * d
                good = jnp.logical_and(so >= 0, so < outer)
                for way, step in ((2, -di), (3, di)):
                    xs = xi + step
                    valid = jnp.logical_and(good, jnp.logical_and(xs >= 0, xs < inner))
                    s = so * inner + xs
                    arrive(s, valid)
                    if inner > 2:
                        forward(s, way, valid)
    for c in own:
        c.wait()

    gate_full = gate_buf[...].reshape(n * rows, 2 * width)
    down_full = down_buf[...].reshape(n * rows, width)
    u = dot(upstream, down_full)
    pre = dot(recv[:, :feats], gate_full)
    a = pre[:, :width]
    b = pre[:, width:]
    sig = jax.nn.sigmoid(a)
    act = a * sig
    hidden = (act * b).astype(BF)
    hid_buf[me] = hidden
    for k in range(1, n):
        peer(hid_buf, hid_buf, h_send, h_recv, k, False).start()
    d_hid = gates * u
    d_pre = jnp.concatenate(
        [d_hid * b * sig * (1.0 + a * (1.0 - sig)), d_hid * act], axis=1).astype(BF)
    ret[:, :feats] = dot(d_pre, gate_full, ((1,), (1,))).astype(BF)
    grad = jnp.sum(hidden.astype(F32) * u, axis=1, keepdims=True)
    ret[:, feats:] = jnp.broadcast_to(grad, (slots, LANES)).astype(BF)
    for k in range(1, groups):
        swap(ret, back, b_send, b_recv, k).start()
    back[block(mine), :] = ret[block(mine), :]

    for k in range(1, groups):
        swap(ret, back, b_send, b_recv, k).wait_recv()
    pick_b = pick.astype(BF)
    o_tok[...] = dot(pick_b, back[:, :feats]).astype(BF)
    slot_g = back[:, feats:]
    lane = lax.broadcasted_iota(jnp.int32, (t_rows, LANES), 1)
    total = jnp.zeros((t_rows, LANES), F32)
    for k in range(topk):
        got = dot(jnp.where(hits[k], pick, 0.0).astype(BF), slot_g)
        total = jnp.where(lane == k, got, total)
    o_gates[...] = total[:, :topk].astype(BF)

    o_down[0] = dot(dx_buf[me], hid_buf[me], ((0,), (0,)))
    for k in range(1, n):
        s = lax.rem(me - k + n, n)
        peer(dx_send, dx_buf, x_send, x_recv, k, True).wait_recv()
        peer(hid_buf, hid_buf, h_send, h_recv, k, False).wait_recv()
        o_down[0] += dot(dx_buf[s], hid_buf[s], ((0,), (0,)))

    for ok, s, way, is_own in started:
        @pl.when(ok)
        def _(s=s, way=way, is_own=is_own):
            for w in range(2):
                hop(w, s, way, is_own).wait_send()
    for k in range(1, groups):
        swap(send, recv, s_send, s_recv, k).wait_send()
        swap(ret, back, b_send, b_recv, k).wait_send()
    for k in range(1, n):
        peer(dx_send, dx_buf, x_send, x_recv, k, True).wait_send()
        peer(hid_buf, hid_buf, h_send, h_recv, k, False).wait_send()


def solution(mesh):
    groups = mesh.shape["expert"]
    n = mesh.shape["dp"]
    inner = 1
    while n % (inner * 2) == 0 and (inner * 2) ** 2 <= n:
        inner *= 2
    outer = n // inner

    def on_device(tokens, d_output, expert_ids, gate_scores, gate_up_w, down_w):
        feats = tokens.shape[1]
        rows = gate_up_w.shape[1]
        width = down_w.shape[2]
        slots = groups * PAD
        vmem = pl.BlockSpec(memory_space=pltpu.VMEM)
        dma = pltpu.SemaphoreType.DMA
        return pl.pallas_call(
            functools.partial(kernel, groups, outer, inner),
            out_shape=(
                jax.ShapeDtypeStruct(tokens.shape, BF),
                jax.ShapeDtypeStruct(gate_scores.shape, BF),
                jax.ShapeDtypeStruct(down_w.shape, F32),
            ),
            in_specs=[vmem] * 6,
            out_specs=(vmem,) * 3,
            scratch_shapes=[
                pltpu.VMEM((n, rows, 2 * width), BF),
                pltpu.VMEM((n, rows, width), BF),
                pltpu.VMEM((slots, 2 * feats + LANES), BF),
                pltpu.VMEM((slots, 2 * feats + LANES), BF),
                pltpu.VMEM((n, slots, width), BF),
                pltpu.VMEM((n, slots, rows), BF),
                pltpu.VMEM((n, slots, rows), BF),
                pltpu.VMEM((slots, feats + LANES), BF),
                pltpu.VMEM((slots, feats + LANES), BF),
                dma((2, 4, n)), dma((2, n)), dma((2,)),
                dma((groups,)), dma((groups,)),
                dma((n,)), dma((n,)),
                dma((n,)), dma((n,)),
                dma((groups,)), dma((groups,)),
            ],
            compiler_params=pltpu.CompilerParams(
                collective_id=0, has_side_effects=True, vmem_limit_bytes=60 * 2**20),
        )(tokens, d_output, expert_ids, gate_scores, gate_up_w, down_w)

    tok = P(("expert", "dp"), None)
    w = P("expert", "dp", None)
    return jax.shard_map(
        on_device, mesh=mesh, in_specs=(tok, tok, tok, tok, w, w),
        out_specs=(tok, tok, w), check_vma=False)
```

time: 152 us -> 53.7 us (0.35)
  Pallas kernels: 0 us -> 46.8 us
  blocking collectives: 34.6 us -> 0 us
  other arithmetic: 32.9 us -> 0 us
  waiting for transfers between devices: 31.6 us -> 0 us
  starting transfers between devices: 17.5 us -> 0 us
  between operations: 14.3 us -> 0.65 us
  local copies, waits for them, and re-layouts: 14.1 us -> 5.93 us
  matrix products: 6.16 us -> 0 us
    pallas_call x0 -> x1, Pallas kernels: none -> 46.8 us  [on_device(): pl.pallas_call(functools.partial(kernel, groups, outer, inner), out_shape...]
    all_gather x1 -> x0, blocking collectives: 34.6 us -> none  [on_device(): lax.all_gather(down_w, 'dp', axis=1, tiled=True)]
    gather x4 -> x0, other arithmetic: 30.6 us -> none  [the longest x3 30.6 us: on_device(): gathered_grads = back_grads[jnp.minimum(slot_of, slot_count - 1)]]
    reduce_scatter x1 -> x0, waiting for transfers between devices: 19.6 us -> none  [on_device(): lax.psum_scatter(transpose_product(d_expert_out, hidden), 'dp', scatter_d...]
    all_to_all x5 -> x0, starting transfers between devices: 17.5 us -> none  [the longest x1 4.26 us: on_device(): lax.all_to_all(send_gates.reshape(groups, CAP), 'expert', split_axis=0, c...]
    all_to_all x5 -> x0, waiting for transfers between devices: 11.2 us -> none  [the longest x1 4.46 us: on_device(): lax.all_to_all(send_upstream.reshape(groups, CAP, features), 'expert', sp...]
    dot_general x8 -> x0, matrix products: 6.16 us -> none  [the longest x2 2.66 us: transpose_product(): lax.dot_general(left, right, (((0,), (0,)), ((), ())), preferred_element_...]
    scatter x1 -> x0, local copies, waits for them, and re-layouts: 4.3 us -> none  [on_device(): owner = jnp.full((slot_count,), -1, jnp.int32).at[slot_of].set(jnp.arange...]
  transfers between devices with their start and end apart: 7 -> 0, of which waited for: 4 -> 0; matrix products, arithmetic and copies ran while one was open for 32% -> 0% of each run, Pallas kernels for 0% -> 0%
where the time goes in v1:
time: 53.7 us; the launch traced here: 53.4 us
  Pallas kernels  46.8 us (87%)
  local copies, waits for them, and re-layouts  5.93 us (11%)
  between operations  0.65 us (1%)
    pallas_call x1, Pallas kernels, on_device(): pl.pallas_call(functools.partial(kernel, groups, outer, inner), out_shape...  46.8 us
    unnamed x8, local copies, waits for them, and re-layouts  4.52 us
    pallas_call x1, local copies, waits for them, and re-layouts, on_device(): pl.pallas_call(functools.partial(kernel, groups, outer, inner), out_shape...  1.41 us

profile of v1, /device:TPU:0, one launch (start us, length us, event | category | flops | bytes accessed | tf_op | source)
XLA Modules:
  0.0 53.4 jit_solution(12194905349148041856)
XLA Ops:
  0.6 0.0 copy-start.1
  0.6 1.4 %copy.10.scores = bf16[128,8]{1,0:T(8,128)(2,1)} copy(bf16[128,8]{0,1:T(8,128)(2,1)} %param.9) | data formatting | bytes 4096 | tf_op args[3]
  2.0 0.0 copy-done.1
  2.0 0.7 %copy.9.ids = s32[128,8]{1,0:T(8,128)} copy(s32[128,8]{0,1:T(8,128)S(1)} %copy-done.1) | data formatting | bytes 8192 | tf_op args[2]
  2.8 46.8 %shard_map.85 = (bf16[128,1024]{1,0:T(8,128)(2,1)}, bf16[128,8]{1,0:T(8,128)(2,1)}, f32[1,128,384]{2,1,0:T(8,128)}) custom-call(bf16[128,1024]{1,0:T(8,128)(2,1)} %tok.1, bf16[128,1024]{1,0:T(8,128)(2,1)} %dout.1, s32[128,8]{1,0:T(8,128)} %copy.9.ids, bf16[128,8]{1,0:T(8,128)(2,1)} %copy.10.scores, bf16[1,128,768]{2,1,0:T(8,128)(2,1)} %gate_in.1, ...), custom_call_target="tpu_custom_call" | custom-call | tf_op jit(solution)/shard_map/pallas_call | solution.py:230
  49.6 1.4 %copy.11 = bf16[128,8]{0,1:T(8,128)(2,1)} copy(bf16[128,8]{1,0:T(8,128)(2,1)} %get-tuple-element.4) | data formatting | bytes 4096 | tf_op jit(solution)/shard_map/pallas_call | solution.py:230
  51.0 0.0 copy-start
  51.0 1.7 %copy.14 = bf16[128,1024]{1,0:T(8,128)(2,1)} copy(bf16[128,1024]{1,0:T(8,128)(2,1)} %get-tuple-element.9) | data formatting | bytes 524288
  52.7 0.0 copy-done
  52.7 0.7 %copy.15 = f32[1,128,384]{2,1,0:T(8,128)} copy(f32[1,128,384]{2,1,0:T(8,128)S(1)} %copy-done) | data formatting | bytes 393216
Async XLA Ops:
  0.6 1.4 %copy-start.1 = (s32[128,8]{0,1:T(8,128)S(1)}, s32[128,8]{0,1:T(8,128)}, u32[]{:S(2)}) copy-start(s32[128,8]{0,1:T(8,128)} %param.8) | copy-start | bytes 12292
  51.0 1.7 %copy-start = (f32[1,128,384]{2,1,0:T(8,128)S(1)}, f32[1,128,384]{2,1,0:T(8,128)}, u32[]{:S(2)}) copy-start(f32[1,128,384]{2,1,0:T(8,128)} %get-tuple-element.11) | copy-start | bytes 589828

commit v2 on v1

v2 whole, which is shorter than its diff:
```python
import functools

import jax
import jax.numpy as jnp
from jax import lax
from jax.experimental import pallas as pl
from jax.experimental.pallas import tpu as pltpu
from jax.sharding import PartitionSpec as P

CAP = 12
PAD = 16
LANES = 128
BF = jnp.bfloat16
F32 = jnp.float32


def dot(left, right, dims=((1,), (0,))):
    return lax.dot_general(left, right, (dims, ((), ())), preferred_element_type=F32)


def kernel(groups, outer, inner, tok, dout, ids, scores, gate_in, down_in,
           o_tok, o_gates, o_down,
           gate_buf, down_buf, x_ch, up_ch, pre_acc, u_acc, send, recv, hid_buf, dx_send, dx_buf, ret, back,
           w_send, w_recv, own_sem, s_send, s_recv, h_send, h_recv, x_send, x_recv, b_send, b_recv):
    n = outer * inner
    me = lax.axis_index("dp")
    mine = lax.axis_index("expert")
    zo = me // inner
    xi = me - zo * inner
    slots = groups * PAD
    rows = gate_in.shape[1]
    feats = tok.shape[1]
    width = down_in.shape[2]
    ins = (down_in, gate_in)
    bufs = (down_buf, gate_buf)

    barrier = pltpu.get_barrier_semaphore()
    for k in range(1, n):
        pl.semaphore_signal(barrier, inc=1, device_id={"dp": lax.rem(me + k, n)},
                            device_id_type=pl.DeviceIdType.MESH)
    for k in range(1, groups):
        pl.semaphore_signal(barrier, inc=1, device_id={"expert": lax.rem(mine + k, groups)},
                            device_id_type=pl.DeviceIdType.MESH)
    pl.semaphore_wait(barrier, n - 1 + groups - 1)

    def remote(src, dst, ss, rs, **where):
        return pltpu.make_async_remote_copy(
            src_ref=src, dst_ref=dst, send_sem=ss, recv_sem=rs,
            device_id=where, device_id_type=pl.DeviceIdType.MESH)

    def target(way):
        return me + (inner, -inner, 1, -1)[way]

    def can(way):
        return (zo < outer - 1, zo > 0, xi < inner - 1, xi > 0)[way]

    def hop(w, s, way, own=False):
        src = ins[w].at[0] if own else bufs[w].at[s]
        return remote(src, bufs[w].at[s], w_send.at[w, way, s], w_recv.at[w, s], dp=target(way))

    started = []
    accs = (u_acc, pre_acc)
    chunks = (up_ch, x_ch)

    def forward(w, s, way, valid, own=False):
        ok = can(way) if valid is None else jnp.logical_and(can(way), valid)

        @pl.when(ok)
        def _():
            hop(w, s, way, own).start()
        started.append((ok, w, s, way, own))

    def arrive(w, s, valid):
        @pl.when(valid)
        def _():
            hop(w, s, 0).wait_recv()

    def add(w, s, valid):
        @pl.when(valid)
        def _():
            accs[w][...] += dot(chunks[w][s], bufs[w][s])

    def outer_shards(d):
        return ((0, me - d * inner, zo >= d), (1, me + d * inner, zo + d < outer))

    def outer_step(w, d):
        for way, s, valid in outer_shards(d):
            arrive(w, s, valid)
            for go in (way, 2, 3):
                forward(w, s, go, valid)

    def outer_add(w, d):
        for _, s, valid in outer_shards(d):
            add(w, s, valid)

    def inner_step(w, d):
        for di in range(1, inner):
            for sign in ((1,) if d == 0 else (-1, 1)):
                so = zo + sign * d
                good = jnp.logical_and(so >= 0, so < outer)
                for way, step in ((2, -di), (3, di)):
                    xs = xi + step
                    valid = jnp.logical_and(good, jnp.logical_and(xs >= 0, xs < inner))
                    s = so * inner + xs
                    arrive(w, s, valid)
                    if inner > 2:
                        forward(w, s, way, valid)
                    add(w, s, valid)

    own = [pltpu.make_async_copy(ins[w].at[0], bufs[w].at[me], own_sem.at[w]) for w in range(2)]
    for way in range(4):
        forward(1, me, way, None, own=True)
    for c in own:
        c.start()

    t_rows = tok.shape[0]
    topk = ids.shape[0]
    row = lax.broadcasted_iota(jnp.int32, (slots, t_rows), 0)
    row_e = row // PAD
    row_r = (row - row_e * PAD).astype(F32)
    idv = ids[...]
    scv = scores[...].astype(F32)
    live = jnp.zeros((slots, t_rows), F32)
    gcol = jnp.zeros((slots, t_rows), F32)
    hits = []
    for k in range(topk):
        hit = idv[k:k + 1, :] == row_e
        hits.append(hit)
        live = jnp.where(hit, 1.0, live)
        gcol = jnp.where(hit, scv[k:k + 1, :], gcol)
    upper = (lax.broadcasted_iota(jnp.int32, (t_rows, t_rows), 0)
             < lax.broadcasted_iota(jnp.int32, (t_rows, t_rows), 1))
    rank = dot(live.astype(BF), jnp.where(upper, 1.0, 0.0).astype(BF))
    pick_t = jnp.where(rank == row_r, live, 0.0)
    pick_b = pick_t.astype(BF)
    send[:, 2 * feats:] = jnp.broadcast_to(
        jnp.sum(pick_t * gcol, axis=1, keepdims=True), (slots, LANES)).astype(BF)
    send[:, :feats] = dot(pick_b, tok[...]).astype(BF)
    send[:, feats:2 * feats] = dot(pick_b, dout[...]).astype(BF)

    def block(e):
        return pl.ds(pl.multiple_of(e * PAD, PAD), PAD)

    def swap(src, dst, ss, rs, k):
        e = lax.rem(mine + k, groups)
        return remote(src.at[block(e), :], dst.at[block(mine), :], ss.at[k], rs.at[k], expert=e)

    for k in range(1, groups):
        swap(send, recv, s_send, s_recv, k).start()
    recv[block(mine), :] = send[block(mine), :]
    pick = jnp.transpose(pick_t).astype(BF)

    def peer(src, dst, ss, rs, k, sliced):
        d = lax.rem(me + k, n)
        return remote(src.at[d] if sliced else src.at[me], dst.at[me], ss.at[k], rs.at[k], dp=d)

    if outer > 1:
        outer_step(1, 1)

    packed = groups * CAP
    pr = lax.broadcasted_iota(jnp.int32, (packed, slots), 0)
    pc = lax.broadcasted_iota(jnp.int32, (packed, slots), 1)
    pack = jnp.where(pc == (pr // CAP) * PAD + pr % CAP, 1.0, 0.0).astype(BF)

    for k in range(1, groups):
        swap(send, recv, s_send, s_recv, k).wait_recv()
    gates = recv[:, 2 * feats:2 * feats + 1].astype(F32)
    upstream = recv[:, feats:2 * feats]
    dexp = dot(pack, (gates * upstream.astype(F32)).astype(BF)).astype(BF)
    for d in range(n):
        dx_send[d] = dexp[:, d * rows:(d + 1) * rows]
        x_ch[d] = recv[:, d * rows:(d + 1) * rows]
        up_ch[d] = recv[:, feats + d * rows:feats + (d + 1) * rows]
    for k in range(1, n):
        peer(dx_send, dx_buf, x_send, x_recv, k, True).start()
    dx_buf[me] = dx_send[me]
    pre_acc[...] = dot(x_ch[me], gate_in[0])
    u_acc[...] = dot(up_ch[me], down_in[0])

    for d in range(2, outer):
        outer_step(1, d)
        outer_add(1, d - 1)
    for way in range(2):
        forward(0, me, way, None, own=True)
    if outer > 1:
        outer_add(1, outer - 1)
    for d in range(outer):
        if d == outer - 1:
            for way in range(2, 4):
                forward(0, me, way, None, own=True)
            if outer > 1:
                outer_step(0, 1)
        inner_step(1, d)

    pre = pre_acc[...]
    a = pre[:, :width]
    b = pre[:, width:]
    sig = jax.nn.sigmoid(a)
    act = a * sig
    hidden = (act * b).astype(BF)
    hid_buf[me] = dot(pack, hidden).astype(BF)
    for k in range(1, n):
        peer(hid_buf, hid_buf, h_send, h_recv, k, False).start()

    for d in range(2, outer):
        outer_step(0, d)
    for d in range(1, outer):
        outer_add(0, d)
    for d in range(outer):
        inner_step(0, d)
    for c in own:
        c.wait()

    u = u_acc[...]
    d_hid = gates * u
    d_pre = jnp.concatenate(
        [d_hid * b * sig * (1.0 + a * (1.0 - sig)), d_hid * act], axis=1).astype(BF)
    gate_full = gate_buf[...].reshape(n * rows, 2 * width)
    ret[:, feats:] = jnp.broadcast_to(
        jnp.sum(hidden.astype(F32) * u, axis=1, keepdims=True), (slots, LANES)).astype(BF)
    ret[:, :feats] = dot(d_pre, gate_full, ((1,), (1,))).astype(BF)
    for k in range(1, groups):
        swap(ret, back, b_send, b_recv, k).start()
    back[block(mine), :] = ret[block(mine), :]

    o_down[0] = dot(dx_buf[me], hid_buf[me], ((0,), (0,)))
    for k in range(1, n):
        s = lax.rem(me - k + n, n)
        peer(dx_send, dx_buf, x_send, x_recv, k, True).wait_recv()
        peer(hid_buf, hid_buf, h_send, h_recv, k, False).wait_recv()
        o_down[0] += dot(dx_buf[s], hid_buf[s], ((0,), (0,)))

    for k in range(1, groups):
        swap(ret, back, b_send, b_recv, k).wait_recv()
    o_tok[...] = dot(pick, back[:, :feats]).astype(BF)
    weighted = pick_t * back[:, feats:feats + 1].astype(F32)
    o_gates[...] = jnp.concatenate(
        [jnp.sum(jnp.where(hit, weighted, 0.0), axis=0, keepdims=True) for hit in hits],
        axis=0).astype(BF)

    for ok, w, s, way, is_own in started:
        @pl.when(ok)
        def _(w=w, s=s, way=way, is_own=is_own):
            hop(w, s, way, is_own).wait_send()
    for k in range(1, groups):
        swap(send, recv, s_send, s_recv, k).wait_send()
        swap(ret, back, b_send, b_recv, k).wait_send()
    for k in range(1, n):
        peer(dx_send, dx_buf, x_send, x_recv, k, True).wait_send()
        peer(hid_buf, hid_buf, h_send, h_recv, k, False).wait_send()


def solution(mesh):
    groups = mesh.shape["expert"]
    n = mesh.shape["dp"]
    inner = 1
    while n % (inner * 2) == 0 and (inner * 2) ** 2 <= n:
        inner *= 2
    outer = n // inner

    def on_device(tokens, d_output, expert_ids, gate_scores, gate_up_w, down_w):
        feats = tokens.shape[1]
        rows = gate_up_w.shape[1]
        width = down_w.shape[2]
        slots = groups * PAD
        packed = groups * CAP
        vmem = pl.BlockSpec(memory_space=pltpu.VMEM)
        dma = pltpu.SemaphoreType.DMA
        grads, d_gates, d_down = pl.pallas_call(
            functools.partial(kernel, groups, outer, inner),
            out_shape=(
                jax.ShapeDtypeStruct(tokens.shape, BF),
                jax.ShapeDtypeStruct(gate_scores.shape[::-1], BF),
                jax.ShapeDtypeStruct(down_w.shape, F32),
            ),
            in_specs=[vmem] * 6,
            out_specs=(vmem,) * 3,
            scratch_shapes=[
                pltpu.VMEM((n, rows, 2 * width), BF),
                pltpu.VMEM((n, rows, width), BF),
                pltpu.VMEM((n, slots, rows), BF),
                pltpu.VMEM((n, slots, rows), BF),
                pltpu.VMEM((slots, 2 * width), F32),
                pltpu.VMEM((slots, width), F32),
                pltpu.VMEM((slots, 2 * feats + LANES), BF),
                pltpu.VMEM((slots, 2 * feats + LANES), BF),
                pltpu.VMEM((n, packed, width), BF),
                pltpu.VMEM((n, packed, rows), BF),
                pltpu.VMEM((n, packed, rows), BF),
                pltpu.VMEM((slots, feats + LANES), BF),
                pltpu.VMEM((slots, feats + LANES), BF),
                dma((2, 4, n)), dma((2, n)), dma((2,)),
                dma((groups,)), dma((groups,)),
                dma((n,)), dma((n,)),
                dma((n,)), dma((n,)),
                dma((groups,)), dma((groups,)),
            ],
            compiler_params=pltpu.CompilerParams(
                collective_id=0, has_side_effects=True, vmem_limit_bytes=60 * 2**20),
        )(tokens, d_output, expert_ids.T, gate_scores.T, gate_up_w, down_w)
        return grads, d_gates.T, d_down

    tok = P(("expert", "dp"), None)
    w = P("expert", "dp", None)
    return jax.shard_map(
        on_device, mesh=mesh, in_specs=(tok, tok, tok, tok, w, w),
        out_specs=(tok, tok, w), check_vma=False)
```

time: 53.7 us -> 50.3 us (0.937)
  local copies, waits for them, and re-layouts: 5.93 us -> 2.97 us
    unnamed x8 -> x7, local copies, waits for them, and re-layouts: 4.52 us -> 2.97 us
    pallas_call x1 -> x0, local copies, waits for them, and re-layouts: 1.41 us -> none  [on_device(): pl.pallas_call(functools.partial(kernel, groups, outer, inner), out_shape...]
where the time goes in v2:
time: 50.3 us; the launch traced here: 50.2 us
  Pallas kernels  46.6 us (93%)
  local copies, waits for them, and re-layouts  2.97 us (6%)
  between operations  0.66 us (1%)
    pallas_call x1, Pallas kernels, on_device(): pl.pallas_call(functools.partial(kernel, groups, outer, inner), out_shape...  46.6 us
    unnamed x7, local copies, waits for them, and re-layouts  2.97 us

profile of v2, /device:TPU:0, one launch (start us, length us, event | category | flops | bytes accessed | tf_op | source)
XLA Modules:
  0.0 50.2 jit_solution(6094730670454905970)
XLA Ops:
  0.6 46.6 %shard_map.85 = (bf16[128,1024]{1,0:T(8,128)(2,1)}, bf16[8,128]{1,0:T(8,128)(2,1)}, f32[1,128,384]{2,1,0:T(8,128)}) custom-call(bf16[128,1024]{1,0:T(8,128)(2,1)} %tok.1, bf16[128,1024]{1,0:T(8,128)(2,1)} %dout.1, s32[8,128]{1,0:T(8,128)} %bitcast.3, bf16[8,128]{1,0:T(8,128)(2,1)} %bitcast.4, bf16[1,128,768]{2,1,0:T(8,128)(2,1)} %gate_in.1, ...), custom_call_target="tpu_custom_call" | custom-call | tf_op jit(solution)/shard_map/pallas_call | solution.py:269
  47.2 0.0 copy-start.1
  47.2 0.0 copy-start
  47.2 1.7 %copy.12 = bf16[128,1024]{1,0:T(8,128)(2,1)} copy(bf16[128,1024]{1,0:T(8,128)(2,1)} %get-tuple-element.12) | data formatting | bytes 524288
  48.9 0.0 copy-done.1
  48.9 0.6 %copy.13 = bf16[128,8]{0,1:T(8,128)(2,1)} copy(bf16[128,8]{0,1:T(8,128)(2,1)S(1)} %bitcast.5) | data formatting | bytes 4096
  49.5 0.0 copy-done
  49.5 0.7 %copy.14 = f32[1,128,384]{2,1,0:T(8,128)} copy(f32[1,128,384]{2,1,0:T(8,128)S(1)} %copy-done) | data formatting | bytes 393216
Async XLA Ops:
  47.2 1.7 %copy-start.1 = (bf16[8,128]{1,0:T(8,128)(2,1)S(1)}, bf16[8,128]{1,0:T(8,128)(2,1)}, u32[]{:S(2)}) copy-start(bf16[8,128]{1,0:T(8,128)(2,1)} %get-tuple-element.7) | copy-start | bytes 6148
  47.2 2.3 %copy-start = (f32[1,128,384]{2,1,0:T(8,128)S(1)}, f32[1,128,384]{2,1,0:T(8,128)}, u32[]{:S(2)}) copy-start(f32[1,128,384]{2,1,0:T(8,128)} %get-tuple-element.14) | copy-start | bytes 589828

commit v3 on v2

--- a/solution.py
+++ b/solution.py
@@ -110,6 +110,8 @@
     own = [pltpu.make_async_copy(ins[w].at[0], bufs[w].at[me], own_sem.at[w]) for w in range(2)]
     for way in range(4):
         forward(1, me, way, None, own=True)
+    for way in range(4):
+        forward(0, me, way, None, own=True)
     for c in own:
         c.start()
 
@@ -156,6 +158,7 @@
 
     if outer > 1:
         outer_step(1, 1)
+        outer_step(0, 1)
 
     packed = groups * CAP
     pr = lax.broadcasted_iota(jnp.int32, (packed, slots), 0)
@@ -179,18 +182,16 @@
 
     for d in range(2, outer):
         outer_step(1, d)
+        outer_step(0, d)
         outer_add(1, d - 1)
-    for way in range(2):
-        forward(0, me, way, None, own=True)
+        outer_add(0, d - 1)
+    for d in range(outer - 1):
+        inner_step(1, d)
+        inner_step(0, d)
     if outer > 1:
         outer_add(1, outer - 1)
-    for d in range(outer):
-        if d == outer - 1:
-            for way in range(2, 4):
-                forward(0, me, way, None, own=True)
-            if outer > 1:
-                outer_step(0, 1)
-        inner_step(1, d)
+        outer_add(0, outer - 1)
+    inner_step(1, outer - 1)
 
     pre = pre_acc[...]
     a = pre[:, :width]
@@ -202,12 +203,7 @@
     for k in range(1, n):
         peer(hid_buf, hid_buf, h_send, h_recv, k, False).start()
 
-    for d in range(2, outer):
-        outer_step(0, d)
-    for d in range(1, outer):
-        outer_add(0, d)
-    for d in range(outer):
-        inner_step(0, d)
+    inner_step(0, outer - 1)
     for c in own:
         c.wait()
 
@@ -248,6 +244,11 @@
     for k in range(1, n):
         peer(dx_send, dx_buf, x_send, x_recv, k, True).wait_send()
         peer(hid_buf, hid_buf, h_send, h_recv, k, False).wait_send()
+
+
+def place(*refs):
+    for src, dst in zip(refs[:3], refs[3:]):
+        dst[...] = src[...]
 
 
 def solution(mesh):
@@ -298,6 +299,12 @@
             compiler_params=pltpu.CompilerParams(
                 collective_id=0, has_side_effects=True, vmem_limit_bytes=60 * 2**20),
         )(tokens, d_output, expert_ids.T, gate_scores.T, gate_up_w, down_w)
+        grads, d_gates, d_down = pl.pallas_call(
+            place,
+            out_shape=tuple(jax.ShapeDtypeStruct(v.shape, v.dtype) for v in (grads, d_gates, d_down)),
+            in_specs=[vmem] * 3,
+            out_specs=(vmem,) * 3,
+        )(grads, d_gates, d_down)
         return grads, d_gates.T, d_down
 
     tok = P(("expert", "dp"), None)

time: 50.3 us -> 44.9 us (0.89)
  local copies, waits for them, and re-layouts: 2.97 us -> 0 us
  Pallas kernels: 46.6 us -> 44.1 us
    pallas_call x1, Pallas kernels: 46.6 us -> 42.3 us  [on_device(): pl.pallas_call(functools.partial(kernel, groups, outer, inner), out_shape...]
    unnamed x7 -> x0, local copies, waits for them, and re-layouts: 2.97 us -> none
    pallas_call x0 -> x1, Pallas kernels: none -> 1.79 us  [on_device(): pl.pallas_call(place, out_shape=tuple((jax.ShapeDtypeStruct(v.shape, v.dt...]
where the time goes in v3:
time: 44.9 us; the launch traced here: 44.7 us
  Pallas kernels  44.1 us (98%)
  between operations  0.64 us (1%)
    pallas_call x1, Pallas kernels, on_device(): pl.pallas_call(functools.partial(kernel, groups, outer, inner), out_shape...  42.3 us
    pallas_call x1, Pallas kernels, on_device(): pl.pallas_call(place, out_shape=tuple((jax.ShapeDtypeStruct(v.shape, v.dt...  1.79 us

profile of v3, /device:TPU:0, one launch (start us, length us, event | category | flops | bytes accessed | tf_op | source)
XLA Modules:
  0.0 44.7 jit_solution(12238781066863005829)
XLA Ops:
  0.6 42.3 %shard_map.85 = (bf16[128,1024]{1,0:T(8,128)(2,1)}, bf16[8,128]{1,0:T(8,128)(2,1)}, f32[1,128,384]{2,1,0:T(8,128)}) custom-call(bf16[128,1024]{1,0:T(8,128)(2,1)} %tok.1, bf16[128,1024]{1,0:T(8,128)(2,1)} %dout.1, s32[8,128]{1,0:T(8,128)} %bitcast.3, bf16[8,128]{1,0:T(8,128)(2,1)} %bitcast.4, bf16[1,128,768]{2,1,0:T(8,128)(2,1)} %gate_in.1, ...), custom_call_target="tpu_custom_call" | custom-call | tf_op jit(solution)/shard_map/pallas_call | solution.py:270
  42.9 1.8 %shard_map.86 = (bf16[128,1024]{1,0:T(8,128)(2,1)}, bf16[8,128]{1,0:T(8,128)(2,1)}, f32[1,128,384]{2,1,0:T(8,128)}) custom-call(bf16[128,1024]{1,0:T(8,128)(2,1)} %get-tuple-element.9.refs_0_, bf16[8,128]{1,0:T(8,128)(2,1)} %get-tuple-element.10.refs_1_, f32[1,128,384]{2,1,0:T(8,128)} %get-tuple-element.11.refs_2_), custom_call_target="tpu_custom_call" | custom-call | tf_op jit(solution)/shard_map/pallas_call | solution.py:302
